TPU v7x, 32 devices: a whole 2x2x4 slice. The times are simulated.
32 devices in a mesh: worker: 8 (over z, core), tensor: 4 (over y, x).
Axes of the slice: x: 2, y: 2, z: 4, core: 2. Of those that a mesh axis runs over, the one named last changes fastest.
Arguments:
- hidden_rows: bfloat16 [8, 512, 3584], P('worker', 'tensor'), may hold values from -6 to 6
- document_ids: int32 [8, 512], P('worker'), may hold values from 0 to 7, never falling along the last dimension, each value on 1 to 256 neighbouring positions
- cotangent: bfloat16 [8, 16, 64, 512], P('worker', None, 'tensor'), may hold values from -16 to 16
- partner_map: int32 [8], replicated, may hold values from 0 to 7, as said below
- inner_weights: bfloat16 [8, 16, 64, 3584], P('worker', None, 'tensor'), may hold values from -6 to 6
- first_moment: float32 [8, 16, 64, 3584], P('worker', None, 'tensor'), may hold values from -0.00021362305 to 0.00021362305
- second_moment: float32 [8, 16, 64, 3584], P('worker', None, 'tensor'), may hold values from 5e-10 to 5e-09
- outer_weights: bfloat16 [8, 16, 64, 3584], P('worker', None, 'tensor'), may hold values from -6 to 6
- outer_momentum: bfloat16 [8, 16, 64, 3584], P('worker', None, 'tensor'), may hold values from -1.5 to 1.5
Outputs:
- projected: bfloat16 [8, 16, 64, 512], P('worker', None, 'tensor')
- momentum_next: bfloat16 [8, 16, 64, 3584], P('worker', None, 'tensor')
Inputs may be any that keep to these rules, and one draw needn't show every extreme that they name: partner_map is an involution without fixed points: partner_map[partner_map[w]] = w and partner_map[w] != w. document_ids never fall along a sequence.
All inputs are finite; a program needn't handle non-finite values.
Results may differ from a plain program's by a relative error of at most 0.0046.
Values may be sent and summed in bfloat16 or wider, within the bound.
No kernel may reach another device: no remote copies, remote signals or barrier semaphores. Data moves between devices by JAX's collectives and lax.ppermute only.
A program may use at most 128 MiB of HBM per device.

v0:
```python
import math

import jax
import jax.numpy as jnp
from jax import lax
from jax.sharding import PartitionSpec as P

KV_HEADS = 4
PAIRS = 64
BLOCKS = 16


rope_base = 1000000.0
clip_norm = 1.0
learn_rate = 0.5
decay_rate = 0.1
bias_first = 1.0
bias_second = 0.632304575
outer_alpha = 0.5
outer_beta = 0.7
outer_gamma = 0.5


def rope_tables(identity, first_pair, count):
    length = identity.shape[0]
    index = jnp.arange(length, dtype=jnp.int32)
    change = jnp.concatenate([jnp.ones((1,), dtype=bool), identity[1:] != identity[:-1]])
    starts = lax.cummax(jnp.where(change, index, jnp.zeros_like(index)), axis=0)
    position = (index - starts).astype(jnp.float32)
    pairs = (first_pair + jnp.arange(count, dtype=jnp.int32)).astype(jnp.float32)
    freq = jnp.exp(pairs * jnp.float32(-math.log(rope_base) / PAIRS))
    angle = freq[:, None] * position[None, :]
    return (jnp.cos(angle), jnp.sin(angle))


def rotate(values, cosine, sine, forward):
    count, length = (values.shape[1], values.shape[2])
    parts = values.reshape(2, KV_HEADS, 2, count, length)
    first = parts[0, :, 0]
    second = parts[0, :, 1]
    cos_b = cosine[None]
    sin_b = sine[None]
    if forward:
        new_first = first * cos_b - second * sin_b
        new_second = second * cos_b + first * sin_b
    else:
        new_first = first * cos_b + second * sin_b
        new_second = second * cos_b - first * sin_b
    keys = jnp.stack([new_first, new_second], axis=1)
    return jnp.concatenate([keys[None], parts[1:2]], axis=0).reshape(BLOCKS, count, length)


def split_rows(values, count):
    return values.reshape(count, values.shape[0] // count, values.shape[1])


def swap_both(pseudo, outer, partner_map):
    count = lax.axis_size("worker")
    spread = (
        lax.all_to_all(
            split_rows(pseudo, count), "worker", split_axis=0, concat_axis=0, tiled=True
        ),
        lax.all_to_all(split_rows(outer, count), "worker", split_axis=0, concat_axis=0, tiled=True),
    )
    routed = (jnp.take(spread[0], partner_map, axis=0), jnp.take(spread[1], partner_map, axis=0))
    back = (
        lax.all_to_all(routed[0], "worker", split_axis=0, concat_axis=0, tiled=True),
        lax.all_to_all(routed[1], "worker", split_axis=0, concat_axis=0, tiled=True),
    )
    return (back[0].reshape(pseudo.shape), back[1].reshape(outer.shape))


def per_device(
    hidden_rows,
    document_ids,
    cotangent,
    partner_map,
    inner_weights,
    first_moment,
    second_moment,
    outer_weights,
    outer_momentum,
):
    local_pairs = cotangent.shape[2]
    length = cotangent.shape[3]
    width = hidden_rows.shape[2]
    columns = BLOCKS * local_pairs
    scale = width ** (-0.5)
    outer = outer_weights[0].reshape(columns, width)
    first_pair = lax.axis_index("tensor") * local_pairs
    cosine, sine = rope_tables(document_ids[0], first_pair, local_pairs)
    dz = (
        rotate(cotangent[0].astype(jnp.float32), cosine, sine, False)
        .astype(jnp.bfloat16)
        .reshape(columns, length)
    )
    weights = inner_weights[0].reshape(columns, width)
    gathered = lax.all_gather(hidden_rows[0], "tensor", axis=0, tiled=True)
    raw = lax.dot_general(
        weights, gathered, (((1,), (1,)), ((), ())), preferred_element_type=jnp.float32
    )
    grad = jnp.dot(dz, gathered, preferred_element_type=jnp.float32)
    raw = raw * scale
    projected = rotate(raw.reshape(BLOCKS, local_pairs, length), cosine, sine, True).astype(
        jnp.bfloat16
    )
    grad = grad * scale
    total = lax.psum(jnp.sum(grad * grad), "tensor")
    factor = jnp.minimum(jnp.float32(1.0), clip_norm / (jnp.sqrt(total) + 1e-06))
    clipped = grad * factor
    moment_new = 0.9 * first_moment[0].reshape(columns, width) + 0.1 * clipped
    second_new = 0.999 * second_moment[0].reshape(columns, width) + 0.001 * clipped * clipped
    update = moment_new / bias_first / (jnp.sqrt(second_new / bias_second) + 1e-08)
    old = weights.astype(jnp.float32)
    theta_new = old - learn_rate * (update + decay_rate * old)
    pseudo = (outer.astype(jnp.float32) - theta_new).astype(jnp.bfloat16)
    pseudo_mate, outer_mate = swap_both(pseudo, outer, partner_map)
    outer_own = outer.astype(jnp.float32)
    moment = outer_momentum[0].reshape(columns, width).astype(jnp.float32)
    result = (
        outer_alpha * moment
        - outer_beta * (pseudo.astype(jnp.float32) + pseudo_mate.astype(jnp.float32)) / 2.0
        - outer_gamma * (outer_own - outer_mate.astype(jnp.float32)) / 2.0
    )
    return (
        projected.reshape(1, BLOCKS, local_pairs, length),
        result.astype(jnp.bfloat16).reshape(1, BLOCKS, local_pairs, width),
    )


def solution(mesh):
    return jax.shard_map(
        per_device,
        mesh=mesh,
        in_specs=(
            P("worker", "tensor", None),
            P("worker", None),
            P("worker", None, "tensor", None),
            P(),
            P("worker", None, "tensor", None),
            P("worker", None, "tensor", None),
            P("worker", None, "tensor", None),
            P("worker", None, "tensor", None),
            P("worker", None, "tensor", None),
        ),
        out_specs=(P("worker", None, "tensor", None), P("worker", None, "tensor", None)),
        check_vma=False,
    )
```

profile of v0, /device:TPU:0, one launch (start us, length us, event | category | flops | bytes accessed | tf_op | source)
XLA Modules:
  0.0 247.9 jit_solution(11799031997270396838)
XLA Ops:
  7.2 0.7 all-gather.3.cloned.1.call-update
  7.9 6.4 %all-to-all-start.2 = ((bf16[8,32,3584]{2,1,0:T(8,128)(2,1)}), bf16[8,32,3584]{2,1,0:T(8,128)(2,1)}, u32[]{:S(2)}, u32[]{:S(2)}) async-start(bf16[8,32,3584]{2,1,0:T(8,128)(2,1)} %bitcast.85), calls=%async_computation.2 | async-start | bytes 3670016 | tf_op jit(solution)/shard_map/all_to_all | solution.py:63
  14.3 0.1 compare_reduce_fusion
  14.4 0.1 add_select_fusion
  14.5 0.3 reduce-window.9
  14.9 0.1 slice_reduce_fusion
  15.0 7.5 %broadcast_multiply_fusion = (f32[1,16,16,3584]{3,2,1,0:T(8,128)}, f32[1,16,16,3584]{3,2,1,0:T(8,128)}) fusion(f32[1,16,16,3584]{3,2,1,0:T(8,128)} %param.17, f32[1,16,16,3584]{3,2,1,0:T(8,128)} %param.16), kind=kLoop, calls=%fused_computation.28 | loop fusion | flops 1835008 | bytes 14680064 | tf_op jit(solution)/shard_map/mul | solution.py:112
  22.6 0.2 multiply_cosine_fusion
  22.9 37.9 %all-gather.3.cloned.1.call-done = bf16[1,512,3584]{2,1,0:T(8,128)(2,1)} async-done(((bf16[1,128,3584]{2,1,0:T(8,128)(2,1)}), bf16[1,512,3584]{2,1,0:T(8,128)(2,1)}) %all-gather.3.cloned.1.call-update) | async-done | bytes 3670032 | tf_op jit(solution)/shard_map/all_gather | solution.py:98
  60.8 3.3 %fusion.17 = f32[256,512]{1,0:T(8,128)S(1)} fusion(bf16[256,3584]{1,0:T(8,128)(2,1)S(1)} %bitcast.87, bf16[1,512,3584]{2,1,0:T(8,128)(2,1)} %all-gather.3.cloned.1.call-done), kind=kOutput, calls=%fused_computation.32 | convolution fusion | flops 939655168 | bytes 6029312 | tf_op jit(solution)/shard_map/dot_general | solution.py:99
  64.3 3.5 %multiply_reduce_fusion = (f32[]{:T(128)}, f32[256,3584]{1,0:T(8,128)}) fusion(bf16[256,512]{1,0:T(8,128)(2,1)S(1)} %bitcast.94, bf16[1,512,3584]{2,1,0:T(8,128)(2,1)S(1)} %copy-done.4), kind=kOutput, calls=%fused_computation.26 | convolution fusion | flops 942276608 | bytes 7602180 | tf_op jit(solution)/shard_map/dot_general | solution.py:102
  67.8 9.5 %psum.7 = f32[]{:T(128)} all-reduce(f32[]{:T(128)} %get-tuple-element.13), channel_id=1, replica_groups=mesh['worker'=8,'tensor'=4] {'tensor'}, use_global_device_ids=true, to_apply=%region_3.4 | all-reduce | flops 1 | bytes 8 | tf_op jit(solution)/shard_map/psum | solution.py:108
  78.1 7.1 %fusion.2 = bf16[256,3584]{1,0:T(8,128)(2,1)} fusion(f32[1,16,16,3584]{3,2,1,0:T(8,128)} %get-tuple-element.17, f32[1,16,16,3584]{3,2,1,0:T(8,128)} %get-tuple-element.18, f32[256,3584]{1,0:T(8,128)} %get-tuple-element.14, bf16[1,16,16,3584]{3,2,1,0:T(8,128)(2,1)S(1)} %copy-done, f32[]{:T(128)S(6)} %mul.231, bf16[1,16,16,3584]{3,2,1,0:T(8,128)(2,1)} %param.15), kind=kLoop, calls=%fused_computation.9 | loop fusion | flops 15597568 | bytes 16515076 | tf_op jit(solution)/shard_map/convert_element_type | solution.py:116
  85.2 4.6 %all-to-all-start = ((bf16[8,32,3584]{2,1,0:T(8,128)(2,1)}), bf16[8,32,3584]{2,1,0:T(8,128)(2,1)}, u32[]{:S(2)}, u32[]{:S(2)}) async-start(bf16[8,32,3584]{2,1,0:T(8,128)(2,1)} %bitcast.86), calls=%async_computation | async-start | bytes 3670016 | tf_op jit(solution)/shard_map/all_to_all | solution.py:60
  89.9 3.4 %gather_fusion.1 = bf16[8,32,3584]{2,1,0:T(8,128)(2,1)} fusion(bf16[8,32,3584]{2,1,0:T(8,128)(2,1)} %all-to-all-done.2, s32[1024]{0:T(1024)S(1)} %pad_clamp_fusion), kind=kCustom, calls=%fused_computation.1.clone | custom fusion | bytes 3670048 | tf_op jit(solution)/shard_map/jit(_take)/gather | solution.py:65
  93.3 40.1 %all-to-all-done = bf16[8,32,3584]{2,1,0:T(8,128)(2,1)} async-done(((bf16[8,32,3584]{2,1,0:T(8,128)(2,1)}), bf16[8,32,3584]{2,1,0:T(8,128)(2,1)}, u32[]{:S(2)}, u32[]{:S(2)}) %all-to-all-start) | async-done | bytes 1835040 | tf_op jit(solution)/shard_map/all_to_all | solution.py:60
  133.4 3.5 %gather_fusion = bf16[8,32,3584]{2,1,0:T(8,128)(2,1)} fusion(bf16[8,32,3584]{2,1,0:T(8,128)(2,1)} %all-to-all-done, s32[1024]{0:T(1024)S(1)} %pad_clamp_fusion), kind=kCustom, calls=%fused_computation.clone | custom fusion | bytes 3670048 | tf_op jit(solution)/shard_map/jit(_take)/gather | solution.py:65
  136.8 3.7 %broadcast_select_fusion.1 = (bf16[8,32,3584]{2,1,0:T(8,128)(2,1)S(1)}, bf16[8,32,3584]{2,1,0:T(8,128)(2,1)}) fusion(bf16[8,32,3584]{2,1,0:T(8,128)(2,1)} %gather_fusion, pred[8]{0:T(512)(128)(4,1)S(1)} %compare_and_fusion, bf16[8,32,3584]{2,1,0:T(8,128)(2,1)} %gather_fusion.1), kind=kLoop, calls=%fused_computation.31 | loop fusion | flops 1835008 | bytes 7340040 | tf_op jit(solution)/shard_map/jit(_take)/select_n | solution.py:65
  140.6 46.6 %all_to_all.20 = bf16[8,32,3584]{2,1,0:T(8,128)(2,1)} all-to-all(bf16[8,32,3584]{2,1,0:T(8,128)(2,1)S(1)} %get-tuple-element.11), channel_id=1, replica_groups=mesh['worker'=8,'tensor'=4] {'worker'}, dimensions={0} | all-to-all | bytes 3670016 | tf_op jit(solution)/shard_map/all_to_all | solution.py:67
  187.2 4.3 %all-to-all-start.3 = ((bf16[8,32,3584]{2,1,0:T(8,128)(2,1)}), bf16[8,32,3584]{2,1,0:T(8,128)(2,1)}, u32[]{:S(2)}, u32[]{:S(2)}) async-start(bf16[8,32,3584]{2,1,0:T(8,128)(2,1)} %get-tuple-element.12), calls=%async_computation.3 | async-start | bytes 3670016 | tf_op jit(solution)/shard_map/all_to_all | solution.py:68
  191.5 3.7 %convert_multiply_fusion.1 = f32[1,16,16,3584]{3,2,1,0:T(8,128)} fusion(bf16[1,16,16,3584]{3,2,1,0:T(8,128)(2,1)} %param.19), kind=kLoop, calls=%fused_computation.27 | loop fusion | flops 1835008 | bytes 5505024 | tf_op jit(solution)/shard_map/mul | solution.py:121
  195.2 0.7 pad_maximum_fusion
  195.9 38.9 %all-to-all-done.3 = bf16[8,32,3584]{2,1,0:T(8,128)(2,1)} async-done(((bf16[8,32,3584]{2,1,0:T(8,128)(2,1)}), bf16[8,32,3584]{2,1,0:T(8,128)(2,1)}, u32[]{:S(2)}, u32[]{:S(2)}) %all-to-all-start.3) | async-done | bytes 1835040 | tf_op jit(solution)/shard_map/all_to_all | solution.py:68
  234.9 6.2 %fusion.5 = bf16[256,3584]{1,0:T(8,128)(2,1)} fusion(f32[1,16,16,3584]{3,2,1,0:T(8,128)} %convert_multiply_fusion.1, bf16[256,3584]{1,0:T(8,128)(2,1)} %fusion.2, bf16[8,32,3584]{2,1,0:T(8,128)(2,1)} %all-to-all-done.3, bf16[8,32,3584]{2,1,0:T(8,128)(2,1)} %all_to_all.20, bf16[1,16,16,3584]{3,2,1,0:T(8,128)(2,1)S(1)} %copy-done), kind=kLoop, calls=%fused_computation.12 | loop fusion | flops 10092544 | bytes 12845056 | tf_op jit(solution)/shard_map/convert_element_type | solution.py:127
  (27 shorter events, 0.5 us)
Async XLA Ops:
  7.2 7.1 %copy-start.3 = (s32[1,512]{1,0:T(1,128)S(1)}, s32[1,512]{1,0:T(1,128)}, u32[]{:S(2)}) copy-start(s32[1,512]{1,0:T(1,128)} %param.12) | copy-start | bytes 6148
  7.2 53.6 %all-gather.3.cloned.1.call-start = ((), (), s32[]{:S(2)}) async-start(), calls=%async_computation.4 | async-start | bytes 4587520 | tf_op jit(solution)/shard_map/all_gather | solution.py:98
  7.9 77.3 %all-to-all-start.2 = ((bf16[8,32,3584]{2,1,0:T(8,128)(2,1)}), bf16[8,32,3584]{2,1,0:T(8,128)(2,1)}, u32[]{:S(2)}, u32[]{:S(2)}) async-start(bf16[8,32,3584]{2,1,0:T(8,128)(2,1)} %bitcast.85), calls=%async_computation.2 | async-start | bytes 3670016 | tf_op jit(solution)/shard_map/all_to_all | solution.py:63
  15.0 7.5 %copy-start.2 = (bf16[1,16,16,512]{3,2,1,0:T(8,128)(2,1)S(1)}, bf16[1,16,16,512]{3,2,1,0:T(8,128)(2,1)}, u32[]{:S(2)}) copy-start(bf16[1,16,16,512]{3,2,1,0:T(8,128)(2,1)} %param.13) | copy-start | bytes 786436
  15.0 45.8 %copy-start.1 = (bf16[1,16,16,3584]{3,2,1,0:T(8,128)(2,1)S(1)}, bf16[1,16,16,3584]{3,2,1,0:T(8,128)(2,1)}, u32[]{:S(2)}) copy-start(bf16[1,16,16,3584]{3,2,1,0:T(8,128)(2,1)} %param.15) | copy-start | bytes 5505028
  60.8 3.5 %copy-start.4 = (bf16[1,512,3584]{2,1,0:T(8,128)(2,1)S(1)}, bf16[1,512,3584]{2,1,0:T(8,128)(2,1)}, u32[]{:S(2)}) copy-start(bf16[1,512,3584]{2,1,0:T(8,128)(2,1)} %all-gather.3.cloned.1.call-done) | copy-start | bytes 11010052
  64.3 13.8 %copy-start = (bf16[1,16,16,3584]{3,2,1,0:T(8,128)(2,1)S(1)}, bf16[1,16,16,3584]{3,2,1,0:T(8,128)(2,1)}, u32[]{:S(2)}) copy-start(bf16[1,16,16,3584]{3,2,1,0:T(8,128)(2,1)} %param.18) | copy-start | bytes 5505028
  85.2 4.6 %copy-start.5 = (s32[8]{0:T(128)S(1)}, s32[8]{0:T(128)}, u32[]{:S(2)}) copy-start(s32[8]{0:T(128)} %param.14) | copy-start | bytes 100
  85.2 48.1 %all-to-all-start = ((bf16[8,32,3584]{2,1,0:T(8,128)(2,1)}), bf16[8,32,3584]{2,1,0:T(8,128)(2,1)}, u32[]{:S(2)}, u32[]{:S(2)}) async-start(bf16[8,32,3584]{2,1,0:T(8,128)(2,1)} %bitcast.86), calls=%async_computation | async-start | bytes 3670016 | tf_op jit(solution)/shard_map/all_to_all | solution.py:60
  187.2 47.7 %all-to-all-start.3 = ((bf16[8,32,3584]{2,1,0:T(8,128)(2,1)}), bf16[8,32,3584]{2,1,0:T(8,128)(2,1)}, u32[]{:S(2)}, u32[]{:S(2)}) async-start(bf16[8,32,3584]{2,1,0:T(8,128)(2,1)} %get-tuple-element.12), calls=%async_computation.3 | async-start | bytes 3670016 | tf_op jit(solution)/shard_map/all_to_all | solution.py:68
Sparse Core Ops, SparseCore 0:
  9.8 50.9 all-gather.2
where the time goes:
time: 248 us
  waiting for transfers between devices  118 us (48%)
  blocking collectives  56.1 us (23%)
  other arithmetic  29.9 us (12%)
  starting transfers between devices  15.3 us (6%)
  between operations  14.9 us (6%)
  local copies, waits for them, and re-layouts  7.14 us (3%)
  matrix products  6.86 us (3%)
    all_to_all x1, blocking collectives, swap_both(): lax.all_to_all(routed[0], 'worker', split_axis=0, concat_axis=0, tiled=True)  46.6 us
    all_to_all x1, waiting for transfers between devices, swap_both(): lax.all_to_all(split_rows(pseudo, count), 'worker', split_axis=0, concat_...  40.1 us
    all_to_all x1, waiting for transfers between devices, swap_both(): lax.all_to_all(routed[1], 'worker', split_axis=0, concat_axis=0, tiled=True)  38.9 us
    all_gather x1, waiting for transfers between devices, per_device(): gathered = lax.all_gather(hidden_rows[0], 'tensor', axis=0, tiled=True)  37.9 us
    psum x1, blocking collectives, per_device(): total = lax.psum(jnp.sum(grad * grad), 'tensor')  9.54 us
    mul x1, other arithmetic, per_device(): 0.999 * second_moment[0].reshape(columns, width) + 0.001 * clipped * clipped  7.48 us
    convert_element_type x1, other arithmetic, per_device(): pseudo = (outer.astype(jnp.float32) - theta_new).astype(jnp.bfloat16)  7.09 us
    all_to_all x1, starting transfers between devices, swap_both(): lax.all_to_all(split_rows(outer, count), 'worker', split_axis=0, concat_a...  6.37 us
  transfers between devices with their start and end apart: 4, of which 3 were waited for; matrix products, arithmetic and copies ran while one was open for 12% of the time, Pallas kernels for 0%

commit v1 on v0

v1 whole, which is shorter than its diff:
```python
import functools
import math

import jax
import jax.numpy as jnp
from jax import lax
from jax.experimental import pallas as pl
from jax.experimental.pallas import tpu as pltpu
from jax.sharding import PartitionSpec as P

KV_HEADS = 4
PAIRS = 64
BLOCKS = 16


rope_base = 1000000.0
clip_norm = 1.0
learn_rate = 0.5
decay_rate = 0.1
bias_first = 1.0
bias_second = 0.632304575
outer_alpha = 0.5
outer_beta = 0.7
outer_gamma = 0.5

TILE = 512
ROWS = 16


def rope_tables(identity, first_pair, count):
    length = identity.shape[0]
    index = jnp.arange(length, dtype=jnp.int32)
    change = jnp.concatenate([jnp.ones((1,), dtype=bool), identity[1:] != identity[:-1]])
    starts = lax.cummax(jnp.where(change, index, jnp.zeros_like(index)), axis=0)
    position = (index - starts).astype(jnp.float32)
    pairs = (first_pair + jnp.arange(count, dtype=jnp.int32)).astype(jnp.float32)
    freq = jnp.exp(pairs * jnp.float32(-math.log(rope_base) / PAIRS))
    angle = freq[:, None] * position[None, :]
    return (jnp.cos(angle), jnp.sin(angle))


def rotate(values, cosine, sine, forward):
    count, length = (values.shape[1], values.shape[2])
    parts = values.reshape(2, KV_HEADS, 2, count, length)
    first = parts[0, :, 0]
    second = parts[0, :, 1]
    cos_b = cosine[None]
    sin_b = sine[None]
    if forward:
        new_first = first * cos_b - second * sin_b
        new_second = second * cos_b + first * sin_b
    else:
        new_first = first * cos_b + second * sin_b
        new_second = second * cos_b - first * sin_b
    keys = jnp.stack([new_first, new_second], axis=1)
    return jnp.concatenate([keys[None], parts[1:2]], axis=0).reshape(BLOCKS, count, length)


def send(values, axis, flip):
    return lax.ppermute(values, axis, [(i, i ^ flip) for i in range(lax.axis_size(axis))])


def swap(values, flip, workers):
    return lax.switch(
        flip - 1,
        [functools.partial(send, axis="worker", flip=f) for f in range(1, workers)],
        values,
    )


def adamw(grad, shrink, first, second, weights, outer):
    half = (0.9 * learn_rate) * first + (0.1 * learn_rate * shrink) * grad
    var = (0.999 / bias_second) * second + (0.001 / bias_second * shrink * shrink) * (grad * grad)
    half = half / (bias_first * (var * lax.rsqrt(var) + 1e-08))
    outer_own = outer.astype(jnp.float32)
    keep = (1.0 - learn_rate * decay_rate) * weights.astype(jnp.float32)
    pseudo = (outer_own - keep + half).astype(jnp.bfloat16).astype(jnp.float32)
    a = (0.5 * outer_gamma) * outer_own
    b = (0.5 * outer_beta) * pseudo
    return a - b, a + b


def limits(mib):
    return pltpu.CompilerParams(vmem_limit_bytes=mib << 20)


def assemble(here, pieces, rows):
    own, x_full, y_low, y_high, d_low, d_high = pieces
    shard = rows.shape[0] // 4

    def put(block, start, ref):
        at = pl.multiple_of((here ^ block) * shard + start, 16)
        rows[pl.ds(at, ref.shape[0]), :] = ref[...]

    put(0, 0, own)
    put(1, 0, x_full)
    put(2, 0, y_low)
    put(2, y_low.shape[0], y_high)
    put(3, 0, d_low)
    put(3, d_low.shape[0], d_high)


def gather_kernel(place, dz, *refs):
    *pieces, grad, squares, rows = refs
    assemble(place[0], pieces, rows)
    part = jnp.dot(dz[...], rows[...], preferred_element_type=jnp.float32)
    grad[...] = part
    part = part * part
    part = jnp.sum(part.reshape(part.shape[0] // 8, 8, part.shape[1]), axis=0)

    @pl.when(pl.program_id(0) == 0)
    def _():
        squares[...] = jnp.zeros_like(squares)

    squares[...] += sum(part[:, 128 * i : 128 * (i + 1)] for i in range(part.shape[1] // 128))


def gather_call(place, dz, pieces):
    width = pieces[0].shape[1]
    columns = dz.shape[0]
    tile = width // 4
    return pl.pallas_call(
        gather_kernel,
        grid_spec=pltpu.PrefetchScalarGridSpec(
            num_scalar_prefetch=1,
            grid=(width // tile,),
            in_specs=[pl.BlockSpec(dz.shape, lambda i, p: (0, 0))]
            + [pl.BlockSpec((x.shape[0], tile), lambda i, p: (0, i)) for x in pieces],
            out_specs=[
                pl.BlockSpec((columns, tile), lambda i, p: (0, i)),
                pl.BlockSpec((8, 128), lambda i, p: (0, 0)),
            ],
            scratch_shapes=[pltpu.VMEM((dz.shape[1], tile), jnp.bfloat16)],
        ),
        out_shape=[
            jax.ShapeDtypeStruct((columns, width), jnp.float32),
            jax.ShapeDtypeStruct((8, 128), jnp.float32),
        ],
        compiler_params=limits(16),
        name="assemble",
    )(place, dz, *pieces)


def adamw_kernel(a, b, c, d, grad, first, second, weights, outer, momentum, mine, own, factor, *,
                 scale):
    @pl.when(pl.program_id(0) == 0)
    def _():
        total = jnp.sum(a[...] + b[...] + c[...] + d[...], axis=(0, 1), keepdims=True)
        norm = jnp.sqrt(total * (scale * scale))
        limit = jnp.minimum(jnp.float32(1.0), clip_norm / (norm + 1e-06))
        factor[0] = limit[0, 0] * scale

    shrink = factor[0]

    def step(i, carry):
        at = (slice(None), pl.ds(pl.multiple_of(i * TILE, TILE), TILE))
        mine[at], rest = adamw(grad[at], shrink, first[at], second[at], weights[at], outer[at])
        own[at] = outer_alpha * momentum[at].astype(jnp.float32) - rest
        return carry

    lax.fori_loop(0, grad.shape[1] // TILE, step, 0, unroll=True)


def adamw_call(sums, grad, arrays, row, rows, scale):
    width = grad.shape[1]
    out = jax.ShapeDtypeStruct((rows, width), jnp.float32)
    fixed = pl.BlockSpec((8, 128), lambda i: (0, 0))
    moved = pl.BlockSpec((ROWS, width), lambda i: (i + row // ROWS, 0))
    return pl.pallas_call(
        functools.partial(adamw_kernel, scale=scale),
        grid=(rows // ROWS,),
        in_specs=[fixed] * 4 + [moved] * 6,
        out_specs=[pl.BlockSpec((ROWS, width), lambda i: (i, 0))] * 2,
        out_shape=[out, out],
        scratch_shapes=[pltpu.SMEM((1,), jnp.float32)],
        compiler_params=limits(12),
        name="adamw",
    )(*sums, grad, *arrays)


def project_kernel(place, weights, cosine, sine, *refs, scale):
    *pieces, projected, rows, raw = refs
    assemble(place[0], pieces, rows)
    part = lax.dot_general(
        weights[...], rows[...], (((1,), (1,)), ((), ())), preferred_element_type=jnp.float32
    )

    @pl.when(pl.program_id(0) == 0)
    def _():
        raw[...] = jnp.zeros_like(raw)

    raw[...] += part

    @pl.when(pl.program_id(0) == pl.num_programs(0) - 1)
    def _():
        count = cosine.shape[0]
        c = cosine[...] * scale
        s = sine[...] * scale
        for head in range(KV_HEADS):
            a = slice(2 * head * count, (2 * head + 1) * count)
            b = slice((2 * head + 1) * count, (2 * head + 2) * count)
            projected[a, :] = (raw[a, :] * c - raw[b, :] * s).astype(jnp.bfloat16)
            projected[b, :] = (raw[b, :] * c + raw[a, :] * s).astype(jnp.bfloat16)
        v = slice(2 * KV_HEADS * count, 4 * KV_HEADS * count)
        projected[v, :] = (raw[v, :] * scale).astype(jnp.bfloat16)


def project_call(place, weights, cosine, sine, pieces, scale):
    columns, width = weights.shape
    length = cosine.shape[1]
    fixed = pl.BlockSpec(cosine.shape, lambda i, p: (0, 0))
    moved = [pl.BlockSpec((x.shape[0], TILE), lambda i, p: (0, i)) for x in (weights, *pieces)]
    return pl.pallas_call(
        functools.partial(project_kernel, scale=scale),
        grid_spec=pltpu.PrefetchScalarGridSpec(
            num_scalar_prefetch=1,
            grid=(width // TILE,),
            in_specs=[moved[0], fixed, fixed] + moved[1:],
            out_specs=pl.BlockSpec((columns, length), lambda i, p: (0, 0)),
            scratch_shapes=[
                pltpu.VMEM((length, TILE), jnp.bfloat16),
                pltpu.VMEM((columns, length), jnp.float32),
            ],
        ),
        out_shape=jax.ShapeDtypeStruct((columns, length), jnp.bfloat16),
        compiler_params=limits(12),
        name="project",
    )(place, weights, cosine, sine, *pieces)


def finish(theirs, own, result, start):
    done = (own + theirs.astype(jnp.float32)).astype(jnp.bfloat16)
    return lax.dynamic_update_slice(result, done, (start, 0))


def per_device(
    hidden_rows,
    document_ids,
    cotangent,
    partner_map,
    inner_weights,
    first_moment,
    second_moment,
    outer_weights,
    outer_momentum,
):
    local_pairs = cotangent.shape[2]
    length = cotangent.shape[3]
    width = hidden_rows.shape[2]
    columns = BLOCKS * local_pairs
    scale = width ** (-0.5)
    shards = lax.axis_size("tensor")
    workers = lax.axis_size("worker")
    place = lax.axis_index("tensor")
    me = lax.axis_index("worker")
    flip = jnp.bitwise_xor(me, partner_map[me])

    hidden = hidden_rows[0]
    weights = inner_weights[0].reshape(columns, width)
    outer = outer_weights[0].reshape(columns, width)
    momentum = outer_momentum[0].reshape(columns, width)
    moment_one = first_moment[0].reshape(columns, width)
    moment_two = second_moment[0].reshape(columns, width)
    cosine, sine = rope_tables(document_ids[0], place * local_pairs, local_pairs)
    dz = (
        rotate(cotangent[0].astype(jnp.float32), cosine, sine, False)
        .astype(jnp.bfloat16)
        .reshape(columns, length)
    )

    if shards == 4 and hidden.shape[0] == 128 and local_pairs == 16 and width % TILE == 0:
        cut = 48
        x_full = send(hidden, "tensor", 1)
        y_high = send(hidden[cut:], "tensor", 2)
        y_low = send(hidden[:cut], "tensor", 2)
        d_high = send(y_high, "tensor", 1)
        d_low = send(x_full[:cut], "tensor", 2)
        dz, flip = lax.optimization_barrier((dz, flip))
        pieces = (hidden, x_full, y_low, y_high, d_low, d_high)
        where = place[None].astype(jnp.int32)
        grad, squares = gather_call(where, dz, pieces)
        sums = [squares] + [send(squares, "tensor", f) for f in (1, 2, 3)]
        arrays = (moment_one, moment_two, weights, outer, momentum)
        sizes = (32, columns - 64, 32)
        starts = (0, 32, columns - 32)

        def tail(f, grad, arrays, pieces):
            theirs = []
            owns = []
            for k in range(3):
                mine, own = adamw_call(sums, grad, arrays, starts[k], sizes[k], scale)
                mine = mine.astype(jnp.float16)
                theirs.append(send(mine, "worker", f))
                owns.append(own)
            projected = project_call(where, weights, cosine, sine, pieces, scale)
            result = jnp.zeros((columns, width), jnp.bfloat16)
            for k in range(2):
                result = finish(theirs[k], owns[k], result, starts[k])
            return projected, result, theirs[2], owns[2]

        projected, result, theirs, own = lax.switch(
            flip - 1, [functools.partial(tail, f) for f in range(1, workers)], grad, arrays, pieces
        )
        result = finish(theirs, own, result, starts[2])
    else:
        gathered = lax.all_gather(hidden, "tensor", axis=0, tiled=True)
        raw = lax.dot_general(
            weights, gathered, (((1,), (1,)), ((), ())), preferred_element_type=jnp.float32
        )
        raw = raw * scale
        projected = rotate(raw.reshape(BLOCKS, local_pairs, length), cosine, sine, True)
        projected = projected.astype(jnp.bfloat16)
        grad = jnp.dot(dz, gathered, preferred_element_type=jnp.float32) * scale
        total = lax.psum(jnp.sum(grad * grad), "tensor")
        factor = jnp.minimum(jnp.float32(1.0), clip_norm / (jnp.sqrt(total) + 1e-06))
        mine, rest = adamw(grad, factor, moment_one, moment_two, weights, outer)
        rest = -rest
        theirs = swap(mine.astype(jnp.float16), flip, workers)
        result = outer_alpha * momentum.astype(jnp.float32) + rest + theirs.astype(jnp.float32)
        result = result.astype(jnp.bfloat16)
    return (
        projected.reshape(1, BLOCKS, local_pairs, length),
        result.reshape(1, BLOCKS, local_pairs, width),
    )


def solution(mesh):
    return jax.shard_map(
        per_device,
        mesh=mesh,
        in_specs=(
            P("worker", "tensor", None),
            P("worker", None),
            P("worker", None, "tensor", None),
            P(),
            P("worker", None, "tensor", None),
            P("worker", None, "tensor", None),
            P("worker", None, "tensor", None),
            P("worker", None, "tensor", None),
            P("worker", None, "tensor", None),
        ),
        out_specs=(P("worker", None, "tensor", None), P("worker", None, "tensor", None)),
        check_vma=False,
    )
```

time: 248 us -> 107 us (0.43)
  waiting for transfers between devices: 118 us -> 53.3 us
  blocking collectives: 56.1 us -> 0 us
  other arithmetic: 29.9 us -> 6.73 us
  Pallas kernels: 0 us -> 22.3 us
  between operations: 14.9 us -> 1.38 us
  matrix products: 6.86 us -> 0 us
  local copies, waits for them, and re-layouts: 7.14 us -> 10.1 us
  starting transfers between devices: 15.3 us -> 12.6 us
    all_to_all x3 -> x0, waiting for transfers between devices: 79 us -> none  [the longest x1 40.1 us: swap_both(): lax.all_to_all(split_rows(pseudo, count), 'worker', split_axis=0, concat_...]
    ppermute x0 -> x11, waiting for transfers between devices: none -> 53.3 us  [send(): lax.ppermute(values, axis, [(i, i ^ flip) for i in range(lax.axis_size(ax...]
    all_to_all x1 -> x0, blocking collectives: 46.6 us -> none  [swap_both(): lax.all_to_all(routed[0], 'worker', split_axis=0, concat_axis=0, tiled=True)]
    all_gather x1 -> x0, waiting for transfers between devices: 37.9 us -> none  [per_device(): gathered = lax.all_gather(hidden_rows[0], 'tensor', axis=0, tiled=True)]
    pallas_call x0 -> x5, Pallas kernels: none -> 22.3 us  [the longest x3 11.7 us: adamw_call(): pl.pallas_call(functools.partial(adamw_kernel, scale=scale), grid=(rows /...]
    all_to_all x3 -> x0, starting transfers between devices: 15.3 us -> none  [the longest x1 6.37 us: swap_both(): lax.all_to_all(split_rows(outer, count), 'worker', split_axis=0, concat_a...]
    convert_element_type x2 -> x4, other arithmetic: 13.2 us -> 0.24 us  [the longest x3 0.2 us: tail(): mine = mine.astype(jnp.float16)]
    ppermute x0 -> x11, starting transfers between devices: none -> 12.6 us  [send(): lax.ppermute(values, axis, [(i, i ^ flip) for i in range(lax.axis_size(ax...]
  transfers between devices with their start and end apart: 4 -> 11, of which waited for: 3 -> 6; matrix products, arithmetic and copies ran while one was open for 12% -> 12% of each run, Pallas kernels for 0% -> 6%
where the time goes in v1:
time: 107 us
  waiting for transfers between devices  53.3 us (50%)
  Pallas kernels  22.3 us (21%)
  starting transfers between devices  12.6 us (12%)
  local copies, waits for them, and re-layouts  10.1 us (9%)
  other arithmetic  6.73 us (6%)
  between operations  1.38 us (1%)
    ppermute x11, waiting for transfers between devices, send(): lax.ppermute(values, axis, [(i, i ^ flip) for i in range(lax.axis_size(ax...  53.3 us
    ppermute x11, starting transfers between devices, send(): lax.ppermute(values, axis, [(i, i ^ flip) for i in range(lax.axis_size(ax...  12.6 us
    pallas_call x3, Pallas kernels, adamw_call(): pl.pallas_call(functools.partial(adamw_kernel, scale=scale), grid=(rows /...  11.7 us
    pallas_call x1, Pallas kernels, gather_call(): pl.pallas_call(gather_kernel, grid_spec=pltpu.PrefetchScalarGridSpec(num_...  5.36 us
    pallas_call x1, Pallas kernels, project_call(): pl.pallas_call(functools.partial(project_kernel, scale=scale), grid_spec=...  5.26 us
    dynamic_update_slice x2, other arithmetic, finish(): return lax.dynamic_update_slice(result, done, (start, 0))  3.14 us
    unnamed x30, local copies, waits for them, and re-layouts  2.61 us
  transfers between devices with their start and end apart: 11, of which 6 were waited for; matrix products, arithmetic and copies ran while one was open for 12% of the time, Pallas kernels for 6%

profile of v1, /device:TPU:0, one launch (start us, length us, event | category | flops | bytes accessed | tf_op | source)
XLA Modules:
  0.0 106.6 jit_solution(9274148445898981822)
XLA Ops:
  0.6 3.0 %collective-permute-start.21 = (bf16[128,3584]{1,0:T(8,128)(2,1)}, bf16[128,3584]{1,0:T(8,128)(2,1)S(1)}, u32[]{:S(2)}, u32[]{:S(2)}) collective-permute-start(bf16[128,3584]{1,0:T(8,128)(2,1)} %bitcast.193), channel_id=1, source_target_pairs={{0,1},{1,0},{2,3},{3,2},{4,5},{5,4},{6,7},{7,6},{8,9},{9,8},{10,11... | collective-permute-start | bytes 2752520 | tf_op jit(solution)/shard_map/ppermute | solution.py:60
  3.7 1.8 %slice_bitcast_fusion.1 = bf16[48,3584]{1,0:T(8,128)(2,1)} fusion(bf16[1,128,3584]{2,1,0:T(8,128)(2,1)} %param.16), kind=kLoop, calls=%fused_computation.24 | loop fusion | bytes 688128 | tf_op jit(solution)/shard_map/slice | solution.py:275
  5.4 1.5 %collective-permute-start.22 = (bf16[48,3584]{1,0:T(8,128)(2,1)}, bf16[48,3584]{1,0:T(8,128)(2,1)S(1)}, u32[]{:S(2)}, u32[]{:S(2)}) collective-permute-start(bf16[48,3584]{1,0:T(8,128)(2,1)} %slice_bitcast_fusion.1), channel_id=1, source_target_pairs={{0,2},{1,3},{2,0},{3,1},{4,6},{5,7},{6,4},{7,5},{8,10},{9,11},{10,... | collective-permute-start | bytes 1032200 | tf_op jit(solution)/shard_map/ppermute | solution.py:60
  7.0 1.1 %slice_bitcast_fusion = bf16[80,3584]{1,0:T(8,128)(2,1)S(1)} fusion(bf16[1,128,3584]{2,1,0:T(8,128)(2,1)} %param.16), kind=kLoop, calls=%fused_computation.21 | loop fusion | bytes 1146880 | tf_op jit(solution)/shard_map/slice | solution.py:274
  9.4 18.0 %collective-permute-done.23.refs_3_ = bf16[80,3584]{1,0:T(8,128)(2,1)S(1)} collective-permute-done((bf16[80,3584]{1,0:T(8,128)(2,1)S(1)}, bf16[80,3584]{1,0:T(8,128)(2,1)S(1)}, u32[]{:S(2)}, u32[]{:S(2)}) %collective-permute-start.23) | collective-permute-done | bytes 573472 | tf_op jit(solution)/shard_map/ppermute | solution.py:60
  28.0 1.0 convert.14
  29.8 1.7 %collective-permute-start.24 = (bf16[48,3584]{1,0:T(8,128)(2,1)}, bf16[48,3584]{1,0:T(8,128)(2,1)}, u32[]{:S(2)}, u32[]{:S(2)}) collective-permute-start(bf16[48,3584]{1,0:T(8,128)(2,1)} %slice.59), channel_id=1, source_target_pairs={{0,2},{1,3},{2,0},{3,1},{4,6},{5,7},{6,4},{7,5},{8,10},{9,11},{10,... | collective-permute-start | bytes 1032200 | tf_op jit(solution)/shard_map/ppermute | solution.py:60
  32.2 0.9 slice.50
  33.1 1.3 %dynamic_slice.3 = s32[1]{0:T(128)} dynamic-slice(s32[8]{0:T(128)} %param.19, s32[]{:T(128)S(6)} %select_n.9), dynamic_slice_sizes={1} | dynamic-slice | bytes 12 | tf_op jit(solution)/shard_map/dynamic_slice | solution.py:256
  35.0 0.9 maximum_bitcast_fusion
  36.0 5.1 %collective-permute-done.25.refs_5_ = bf16[80,3584]{1,0:T(8,128)(2,1)S(1)} collective-permute-done((bf16[80,3584]{1,0:T(8,128)(2,1)S(1)}, bf16[80,3584]{1,0:T(8,128)(2,1)S(1)}, u32[]{:S(2)}, u32[]{:S(2)}) %collective-permute-start.25) | collective-permute-done | bytes 573472 | tf_op jit(solution)/shard_map/ppermute | solution.py:60
  41.9 5.4 %assemble.1 = (f32[256,3584]{1,0:T(8,128)}, f32[8,128]{1,0:T(8,128)S(1)}) custom-call(s32[1]{0:T(128)} %bitcast.51.place, bf16[256,512]{1,0:T(8,128)(2,1)S(1)} %bitcast.80, bf16[128,3584]{1,0:T(8,128)(2,1)S(1)} %bitcast.194, bf16[128,3584]{1,0:T(8,128)(2,1)} %copy-done.37, bf16[48,3584]{1,0:T(8,128)(2,1)} %copy-done.53, ...), custom_call_target="tpu_custom_call" | custom-call | tf_op jit(solution)/shard_map/assemble/pallas_call | solution.py:122
  47.8 1.5 %collective-permute-start.27 = (f32[8,128]{1,0:T(8,128)S(1)}, f32[8,128]{1,0:T(8,128)S(1)}, u32[]{:S(2)}, u32[]{:S(2)}) collective-permute-start(f32[8,128]{1,0:T(8,128)S(1)} %get-tuple-element.501), channel_id=1, source_target_pairs={{0,2},{1,3},{2,0},{3,1},{4,6},{5,7},{6,4},{7,5},{8,10},{9,11},{10,... | collective-permute-start | bytes 12296 | tf_op jit(solution)/shard_map/ppermute | solution.py:60
  49.3 1.4 %collective-permute-start.28 = (f32[8,128]{1,0:T(8,128)S(1)}, f32[8,128]{1,0:T(8,128)S(1)}, u32[]{:S(2)}, u32[]{:S(2)}) collective-permute-start(f32[8,128]{1,0:T(8,128)S(1)} %get-tuple-element.501), channel_id=1, source_target_pairs={{0,3},{1,2},{2,1},{3,0},{4,7},{5,6},{6,5},{7,4},{8,11},{9,10},{10,... | collective-permute-start | bytes 12296 | tf_op jit(solution)/shard_map/ppermute | solution.py:60
  51.4 2.4 %collective-permute-done.28 = f32[8,128]{1,0:T(8,128)S(1)} collective-permute-done((f32[8,128]{1,0:T(8,128)S(1)}, f32[8,128]{1,0:T(8,128)S(1)}, u32[]{:S(2)}, u32[]{:S(2)}) %collective-permute-start.28) | collective-permute-done | bytes 4128 | tf_op jit(solution)/shard_map/ppermute | solution.py:60
  53.8 51.0 %conditional.4 = (bf16[256,3584]{1,0:T(8,128)(2,1)}, f32[32,3584]{1,0:T(8,128)S(1)}, bf16[1,16,16,512]{3,2,1,0:T(8,128)(2,1)S(1)}, f16[32,3584]{1,0:T(8,128)(2,1)}) conditional(s32[]{:T(128)} %clamp.3, (f32[1,16,16,3584]{3,2,1,0:T(8,128)}, f32[1,16,16,3584]{3,2,1,0:T(8,128)}, bf16[1,16,16,3584]{3,2,1,0:T(8,128)(2,1)S(1)}, ...), branch_computations={%region_2.3_spmd, %region_3.4_spmd, %region_4.5_spmd, %region_5.6_... | conditional | flops 3325952 | bytes 87490944
  53.8 10.5 %adamw.28 = (f32[192,3584]{1,0:T(8,128)S(1)}, f32[192,3584]{1,0:T(8,128)S(1)}) custom-call(f32[8,128]{1,0:T(8,128)S(1)} %get-tuple-element.369.a, f32[8,128]{1,0:T(8,128)S(1)} %get-tuple-element.370.b, f32[8,128]{1,0:T(8,128)S(1)} %get-tuple-element.371.c, f32[8,128]{1,0:T(8,128)S(1)} %get-tuple-element.372.d, f32[256,3584]{1,0:T(8,128)} %get-tuple-element.373.grad, ...), custom_call_target="tpu_custom_call" | custom-call | tf_op jit(solution)/shard_map/cond/branch_2_fun/adamw/pallas_call | solution.py:169
  64.5 1.8 %copy-done.2 = f32[1,16,16,3584]{3,2,1,0:T(8,128)S(1)} copy-done((f32[1,16,16,3584]{3,2,1,0:T(8,128)S(1)}, f32[1,16,16,3584]{3,2,1,0:T(8,128)}, u32[]{:S(2)}) %copy-start.2) | copy-done | bytes 3670040
  67.7 1.8 %collective-permute-start.8 = (f16[32,3584]{1,0:T(8,128)(2,1)S(1)}, f16[32,3584]{1,0:T(8,128)(2,1)}, u32[]{:S(2)}, u32[]{:S(2)}) collective-permute-start(f16[32,3584]{1,0:T(8,128)(2,1)S(1)} %convert_element_type.160), channel_id=1, source_target_pairs={{0,12},{4,8},{8,4},{12,0},{16,28},{20,24},{24,20},{28,16},{1,13},{... | collective-permute-start | bytes 688136 | tf_op jit(solution)/shard_map/cond/branch_2_fun/ppermute | solution.py:60
  69.7 5.3 %project.9 = bf16[256,512]{1,0:T(8,128)(2,1)S(1)} custom-call(s32[1]{0:T(128)} %get-tuple-element.384.place, bf16[256,3584]{1,0:T(8,128)(2,1)S(1)} %bitcast.134, f32[16,512]{1,0:T(8,128)S(1)} %get-tuple-element.518.cosine, f32[16,512]{1,0:T(8,128)S(1)} %get-tuple-element.517.sine, bf16[128,3584]{1,0:T(8,128)(2,1)S(1)} %get-tuple-element.386.refs_0_, ...), custom_call_target="tpu_custom_call" | custom-call | tf_op jit(solution)/shard_map/cond/branch_2_fun/project/pallas_call | solution.py:213
  74.9 27.1 %collective-permute-done.6 = f16[32,3584]{1,0:T(8,128)(2,1)S(1)} collective-permute-done((f16[32,3584]{1,0:T(8,128)(2,1)S(1)}, f16[32,3584]{1,0:T(8,128)(2,1)S(1)}, u32[]{:S(2)}, u32[]{:S(2)}) %collective-permute-start.6) | collective-permute-done | bytes 229408 | tf_op jit(solution)/shard_map/cond/branch_2_fun/ppermute | solution.py:60
  102.1 1.3 %dynamic_update_slice.34 = bf16[256,3584]{1,0:T(8,128)(2,1)} pad(bf16[32,3584]{1,0:T(8,128)(2,1)S(1)} %add_convert_fusion.5, bf16[]{:T(256)} %constant.27.clone), padding=0_224x0_0 | pad | bytes 2064386 | tf_op jit(solution)/shard_map/cond/branch_2_fun/dynamic_update_slice | solution.py:233
  103.5 1.4 %fusion.2 = bf16[256,3584]{1,0:T(8,128)(2,1)} fusion(bf16[256,3584]{1,0:T(8,128)(2,1)} %dynamic_update_slice.34, f32[192,3584]{1,0:T(8,128)S(1)} %get-tuple-element.381, f16[192,3584]{1,0:T(8,128)(2,1)S(1)} %collective-permute-done.7), kind=kLoop, calls=%fused_computation.7 | loop fusion | flops 2064384 | bytes 5505024 | tf_op jit(solution)/shard_map/cond/branch_2_fun/dynamic_update_slice | solution.py:233
  104.8 1.8 %fusion.8 = bf16[256,3584]{1,0:T(8,128)(2,1)} fusion(bf16[256,3584]{1,0:T(8,128)(2,1)} %get-tuple-element.504, f32[32,3584]{1,0:T(8,128)S(1)} %get-tuple-element.505, f16[32,3584]{1,0:T(8,128)(2,1)} %get-tuple-element.512), kind=kLoop, calls=%fused_computation.26 | loop fusion | flops 344064 | bytes 917504 | tf_op jit(solution)/shard_map/dynamic_update_slice | solution.py:233
  (60 shorter events, 7.3 us)
Async XLA Ops:
  0.6 8.0 %copy-start.62 = (s32[1,512]{1,0:T(1,128)S(1)}, s32[1,512]{1,0:T(1,128)}, u32[]{:S(2)}) copy-start(s32[1,512]{1,0:T(1,128)} %param.17) | copy-start | bytes 6148
  0.6 28.3 %collective-permute-start.21 = (bf16[128,3584]{1,0:T(8,128)(2,1)}, bf16[128,3584]{1,0:T(8,128)(2,1)S(1)}, u32[]{:S(2)}, u32[]{:S(2)}) collective-permute-start(bf16[128,3584]{1,0:T(8,128)(2,1)} %bitcast.193), channel_id=1, source_target_pairs={{0,1},{1,0},{2,3},{3,2},{4,5},{5,4},{6,7},{7,6},{8,9},{9,8},{10,11... | collective-permute-start | bytes 2752520 | tf_op jit(solution)/shard_map/ppermute | solution.py:60
  5.4 30.5 %collective-permute-start.22 = (bf16[48,3584]{1,0:T(8,128)(2,1)}, bf16[48,3584]{1,0:T(8,128)(2,1)S(1)}, u32[]{:S(2)}, u32[]{:S(2)}) collective-permute-start(bf16[48,3584]{1,0:T(8,128)(2,1)} %slice_bitcast_fusion.1), channel_id=1, source_target_pairs={{0,2},{1,3},{2,0},{3,1},{4,6},{5,7},{6,4},{7,5},{8,10},{9,11},{10,... | collective-permute-start | bytes 1032200 | tf_op jit(solution)/shard_map/ppermute | solution.py:60
  8.1 33.8 %copy-start.36 = (bf16[1,128,3584]{2,1,0:T(8,128)(2,1)S(1)}, bf16[1,128,3584]{2,1,0:T(8,128)(2,1)}, u32[]{:S(2)}) copy-start(bf16[1,128,3584]{2,1,0:T(8,128)(2,1)} %param.16) | copy-start | bytes 2752516
  8.1 19.4 %collective-permute-start.23 = (bf16[80,3584]{1,0:T(8,128)(2,1)S(1)}, bf16[80,3584]{1,0:T(8,128)(2,1)S(1)}, u32[]{:S(2)}, u32[]{:S(2)}) collective-permute-start(bf16[80,3584]{1,0:T(8,128)(2,1)S(1)} %slice_bitcast_fusion), channel_id=1, source_target_pairs={{0,2},{1,3},{2,0},{3,1},{4,6},{5,7},{6,4},{7,5},{8,10},{9,11},{10,... | collective-permute-start | bytes 1720328 | tf_op jit(solution)/shard_map/ppermute | solution.py:60
  27.5 13.6 %collective-permute-start.25 = (bf16[80,3584]{1,0:T(8,128)(2,1)S(1)}, bf16[80,3584]{1,0:T(8,128)(2,1)S(1)}, u32[]{:S(2)}, u32[]{:S(2)}) collective-permute-start(bf16[80,3584]{1,0:T(8,128)(2,1)S(1)} %collective-permute-done.23.refs_3_), channel_id=1, source_target_pairs={{0,1},{1,0},{2,3},{3,2},{4,5},{5,4},{6,7},{7,6},{8,9},{9,8},{10,11... | collective-permute-start | bytes 1720328 | tf_op jit(solution)/shard_map/ppermute | solution.py:60
  29.0 12.1 %copy-start.37 = (bf16[128,3584]{1,0:T(8,128)(2,1)}, bf16[128,3584]{1,0:T(8,128)(2,1)S(1)}, u32[]{:S(2)}) copy-start(bf16[128,3584]{1,0:T(8,128)(2,1)S(1)} %collective-permute-done.21.refs_1_) | copy-start | bytes 2752516
  29.8 11.2 %collective-permute-start.24 = (bf16[48,3584]{1,0:T(8,128)(2,1)}, bf16[48,3584]{1,0:T(8,128)(2,1)}, u32[]{:S(2)}, u32[]{:S(2)}) collective-permute-start(bf16[48,3584]{1,0:T(8,128)(2,1)} %slice.59), channel_id=1, source_target_pairs={{0,2},{1,3},{2,0},{3,1},{4,6},{5,7},{6,4},{7,5},{8,10},{9,11},{10,... | collective-permute-start | bytes 1032200 | tf_op jit(solution)/shard_map/ppermute | solution.py:60
  36.0 5.1 %copy-start.53 = (bf16[48,3584]{1,0:T(8,128)(2,1)}, bf16[48,3584]{1,0:T(8,128)(2,1)S(1)}, u32[]{:S(2)}) copy-start(bf16[48,3584]{1,0:T(8,128)(2,1)S(1)} %collective-permute-done.22.refs_2_) | copy-start | bytes 1032196
  41.9 11.9 %copy-start.21 = (bf16[1,16,16,3584]{3,2,1,0:T(8,128)(2,1)S(1)}, bf16[1,16,16,3584]{3,2,1,0:T(8,128)(2,1)}, u32[]{:S(2)}) copy-start(bf16[1,16,16,3584]{3,2,1,0:T(8,128)(2,1)} %param.20) | copy-start | bytes 5505028
  47.2 3.6 %collective-permute-start.26 = (f32[8,128]{1,0:T(8,128)S(1)}, f32[8,128]{1,0:T(8,128)S(1)}, u32[]{:S(2)}, u32[]{:S(2)}) collective-permute-start(f32[8,128]{1,0:T(8,128)S(1)} %get-tuple-element.501), channel_id=1, source_target_pairs={{0,1},{1,0},{2,3},{3,2},{4,5},{5,4},{6,7},{7,6},{8,9},{9,8},{10,11... | collective-permute-start | bytes 12296 | tf_op jit(solution)/shard_map/ppermute | solution.py:60
  47.8 3.6 %collective-permute-start.27 = (f32[8,128]{1,0:T(8,128)S(1)}, f32[8,128]{1,0:T(8,128)S(1)}, u32[]{:S(2)}, u32[]{:S(2)}) collective-permute-start(f32[8,128]{1,0:T(8,128)S(1)} %get-tuple-element.501), channel_id=1, source_target_pairs={{0,2},{1,3},{2,0},{3,1},{4,6},{5,7},{6,4},{7,5},{8,10},{9,11},{10,... | collective-permute-start | bytes 12296 | tf_op jit(solution)/shard_map/ppermute | solution.py:60
  49.3 4.5 %collective-permute-start.28 = (f32[8,128]{1,0:T(8,128)S(1)}, f32[8,128]{1,0:T(8,128)S(1)}, u32[]{:S(2)}, u32[]{:S(2)}) collective-permute-start(f32[8,128]{1,0:T(8,128)S(1)} %get-tuple-element.501), channel_id=1, source_target_pairs={{0,3},{1,2},{2,1},{3,0},{4,7},{5,6},{6,5},{7,4},{8,11},{9,10},{10,... | collective-permute-start | bytes 12296 | tf_op jit(solution)/shard_map/ppermute | solution.py:60
  53.8 10.7 %copy-start.9 = (f32[1,16,16,3584]{3,2,1,0:T(8,128)S(1)}, f32[1,16,16,3584]{3,2,1,0:T(8,128)}, u32[]{:S(2)}) copy-start(f32[1,16,16,3584]{3,2,1,0:T(8,128)} %get-tuple-element.375) | copy-start | bytes 11010052
  53.8 10.7 %copy-start.16 = (f32[256,3584]{1,0:T(8,128)S(1)}, f32[256,3584]{1,0:T(8,128)}, u32[]{:S(2)}) copy-start(f32[256,3584]{1,0:T(8,128)} %get-tuple-element.373.grad) | copy-start | bytes 11010052
  53.8 10.7 %copy-start.24 = (bf16[1,16,16,3584]{3,2,1,0:T(8,128)(2,1)S(1)}, bf16[1,16,16,3584]{3,2,1,0:T(8,128)(2,1)}, u32[]{:S(2)}) copy-start(bf16[1,16,16,3584]{3,2,1,0:T(8,128)(2,1)} %get-tuple-element.377) | copy-start | bytes 5505028
  53.8 10.7 %copy-start.31 = (bf16[1,16,16,3584]{3,2,1,0:T(8,128)(2,1)S(1)}, bf16[1,16,16,3584]{3,2,1,0:T(8,128)(2,1)}, u32[]{:S(2)}) copy-start(bf16[1,16,16,3584]{3,2,1,0:T(8,128)(2,1)} %get-tuple-element.378) | copy-start | bytes 5505028
  64.3 2.0 %copy-start.2 = (f32[1,16,16,3584]{3,2,1,0:T(8,128)S(1)}, f32[1,16,16,3584]{3,2,1,0:T(8,128)}, u32[]{:S(2)}) copy-start(f32[1,16,16,3584]{3,2,1,0:T(8,128)} %get-tuple-element.374) | copy-start | bytes 11010052
  64.4 39.0 %collective-permute-start.7 = (f16[192,3584]{1,0:T(8,128)(2,1)S(1)}, f16[192,3584]{1,0:T(8,128)(2,1)S(1)}, u32[]{:S(2)}, u32[]{:S(2)}) collective-permute-start(f16[192,3584]{1,0:T(8,128)(2,1)S(1)} %convert_element_type.157), channel_id=1, source_target_pairs={{0,12},{4,8},{8,4},{12,0},{16,28},{20,24},{24,20},{28,16},{1,13},{... | collective-permute-start | bytes 4128776 | tf_op jit(solution)/shard_map/cond/branch_2_fun/ppermute | solution.py:60
  66.9 2.7 %copy-start.40 = (bf16[128,3584]{1,0:T(8,128)(2,1)S(1)}, bf16[128,3584]{1,0:T(8,128)(2,1)}, u32[]{:S(2)}) copy-start(bf16[128,3584]{1,0:T(8,128)(2,1)} %get-tuple-element.387.refs_1_) | copy-start | bytes 2752516
  67.0 2.7 %copy-start.48 = (bf16[80,3584]{1,0:T(8,128)(2,1)S(1)}, bf16[80,3584]{1,0:T(8,128)(2,1)}, u32[]{:S(2)}) copy-start(bf16[80,3584]{1,0:T(8,128)(2,1)} %get-tuple-element.391.refs_5_) | copy-start | bytes 1720324
  67.0 2.7 %copy-start.56 = (bf16[48,3584]{1,0:T(8,128)(2,1)S(1)}, bf16[48,3584]{1,0:T(8,128)(2,1)}, u32[]{:S(2)}) copy-start(bf16[48,3584]{1,0:T(8,128)(2,1)} %get-tuple-element.388.refs_2_) | copy-start | bytes 1032196
  67.0 35.1 %collective-permute-start.6 = (f16[32,3584]{1,0:T(8,128)(2,1)S(1)}, f16[32,3584]{1,0:T(8,128)(2,1)S(1)}, u32[]{:S(2)}, u32[]{:S(2)}) collective-permute-start(f16[32,3584]{1,0:T(8,128)(2,1)S(1)} %convert_element_type.154), channel_id=1, source_target_pairs={{0,12},{4,8},{8,4},{12,0},{16,28},{20,24},{24,20},{28,16},{1,13},{... | collective-permute-start | bytes 688136 | tf_op jit(solution)/shard_map/cond/branch_2_fun/ppermute | solution.py:60
  67.7 37.1 %collective-permute-start.8 = (f16[32,3584]{1,0:T(8,128)(2,1)S(1)}, f16[32,3584]{1,0:T(8,128)(2,1)}, u32[]{:S(2)}, u32[]{:S(2)}) collective-permute-start(f16[32,3584]{1,0:T(8,128)(2,1)S(1)} %convert_element_type.160), channel_id=1, source_target_pairs={{0,12},{4,8},{8,4},{12,0},{16,28},{20,24},{24,20},{28,16},{1,13},{... | collective-permute-start | bytes 688136 | tf_op jit(solution)/shard_map/cond/branch_2_fun/ppermute | solution.py:60
  (2 other events, 2.6 us)
